TPU v7x, 32 devices: a whole 2x2x4 slice. The times are simulated.
32 devices in a mesh: tm: 2 (over y), rows: 4 (over z), dp: 4 (over x, core).
Axes of the slice: x: 2, y: 2, z: 4, core: 2. Of those that a mesh axis runs over, the one named last changes fastest.
Arguments:
- video: bfloat16 [4, 32, 16, 32, 128], P('dp', 'tm', 'rows'), may hold values from -6 to 6
- cotangent: bfloat16 [4, 32, 16, 32, 128], P('dp', 'tm', 'rows'), may hold values from -6 to 6
- in_kernel: bfloat16 [3, 3, 128, 128], replicated, may hold values from -0.03125 to 0.03125
- out_kernel: bfloat16 [3, 3, 128, 128], replicated, may hold values from -0.1875 to 0.1875
- skip_gain: float32 [128], replicated, may hold values from 0.5 to 1.5
- log_decay: float32 [32, 128], P('tm'), may hold values from -3 to 0, as said below
Outputs:
- layer_out: bfloat16 [4, 32, 16, 32, 128], P('dp', 'tm', 'rows')
- video_grad: bfloat16 [4, 32, 16, 32, 128], P('dp', 'tm', 'rows')
- in_kernel_grad: float32 [3, 3, 128, 128], replicated
- out_kernel_grad: float32 [3, 3, 128, 128], replicated
- skip_gain_grad: float32 [128], replicated
- decay_grad: float32 [32, 128], P('tm')
Inputs may be any that keep to these rules, and one draw needn't show every extreme that they name: log_decay is negative.
All inputs are finite; a program needn't handle non-finite values.
Results may differ from a plain program's by a relative error of at most 0.0085.
Values may be sent and summed in bfloat16 or wider, within the bound.
No kernel may reach another device: no remote copies, remote signals or barrier semaphores. Data moves between devices by JAX's collectives and lax.ppermute only.
A program may use at most 64 MiB of HBM per device.

v0:
```python
import math
import jax
import jax.numpy as jnp
from jax import lax
from jax.sharding import PartitionSpec as P


def padded_2(cells, sides, width):
    for axis, dim in sides:
        count = lax.axis_size(axis)
        ends = count - 1
        head = lax.slice_in_dim(cells, 0, width, axis=dim)
        tail = lax.slice_in_dim(cells, cells.shape[dim] - width, cells.shape[dim], axis=dim)
        cells = jnp.concatenate(
            [
                lax.ppermute(tail, axis, [(i, (i + 1) % count) for i in range(ends)]),
                cells,
                lax.ppermute(head, axis, [((i + 1) % count, i) for i in range(ends)]),
            ],
            axis=dim,
        )
    return cells


def pad_columns(field):
    return jnp.pad(field, ((0, 0), (0, 0), (0, 0), (1, 1), (0, 0)))


def forward_conv(padded, kernel):
    seqs, frames, rows_two, cols_two, chans = padded.shape
    rows, cols = (rows_two - 2, cols_two - 2)
    total = None
    for i in range(3):
        for j in range(3):
            piece = padded[:, :, i : i + rows, j : j + cols, :].reshape(-1, chans)
            term = jnp.dot(piece, kernel[i, j], preferred_element_type=jnp.float32)
            total = term if total is None else total + term
    return total.reshape(seqs, frames, rows, cols, kernel.shape[3])


def adjoint_conv(padded, kernel):
    seqs, frames, rows_two, cols_two, chans = padded.shape
    rows, cols = (rows_two - 2, cols_two - 2)
    total = None
    for i in range(3):
        for j in range(3):
            piece = padded[:, :, 2 - i : 2 - i + rows, 2 - j : 2 - j + cols, :].reshape(-1, chans)
            term = lax.dot_general(
                piece, kernel[i, j], (((1,), (1,)), ((), ())), preferred_element_type=jnp.float32
            )
            total = term if total is None else total + term
    return total.reshape(seqs, frames, rows, cols, kernel.shape[2])


def kernel_grad(padded, grad):
    seqs, frames, rows_two, cols_two, chans = padded.shape
    rows, cols = (rows_two - 2, cols_two - 2)
    flat_grad = grad.reshape(-1, grad.shape[-1])
    outer_list = []
    for i in range(3):
        inner_list = []
        for j in range(3):
            piece = padded[:, :, i : i + rows, j : j + cols, :].reshape(-1, chans)
            inner_list.append(
                lax.dot_general(
                    piece, flat_grad, (((0,), (0,)), ((), ())), preferred_element_type=jnp.float32
                )
            )
        outer_list.append(jnp.stack(inner_list))
    return jnp.stack(outer_list)


def on_device(video, cotangent, in_kernel, out_kernel, skip_gain, log_decay):
    seqs, frames, rows, cols, chans = video.shape
    padded_x = pad_columns(padded_2(video, (("rows", 2),), 1))
    drive = forward_conv(padded_x, in_kernel)
    cum = jnp.cumsum(log_decay, axis=0)
    later_mask = (
        lax.broadcasted_iota(jnp.int32, (frames, frames), 0)
        >= lax.broadcasted_iota(jnp.int32, (frames, frames), 1)
    )[:, :, None]
    gaps = cum[:, None, :] - cum[None, :, :]
    within = jnp.where(later_mask, jnp.exp(jnp.where(later_mask, gaps, 0.0)), 0.0)
    local_states = jnp.einsum("tkp,skrcp->strcp", within, drive, precision=lax.Precision.HIGHEST)
    group_total = cum[-1]
    empty = jnp.zeros_like(local_states[:, -1])
    group_logs = lax.all_gather(group_total[None, :], "tm", axis=0, tiled=True)
    running = jnp.cumsum(group_logs, axis=0)
    own = lax.axis_index("tm")
    own_running = lax.dynamic_index_in_dim(running, own, 0, keepdims=False)
    piece = lax.all_gather(
        local_states[:, -1][None].astype(jnp.bfloat16), "tm", axis=0, tiled=True
    ).astype(jnp.float32)
    count = piece.shape[0]
    upto = running
    index = jnp.arange(count, dtype=jnp.int32)
    reach = own_running[None, :] - group_total[None, :] - upto
    weight = jnp.where((index < own)[:, None], jnp.exp(jnp.minimum(reach, 0.0)), 0.0)
    carry_in = empty + jnp.einsum("np,nsrcp->srcp", weight, piece, precision=lax.Precision.HIGHEST)
    states = local_states + jnp.exp(cum)[None, :, None, None, :] * carry_in[:, None]
    states_bf = states.astype(jnp.bfloat16)
    padded_s = pad_columns(padded_2(states_bf, (("rows", 2),), 1))
    pre = forward_conv(padded_s, out_kernel) + skip_gain * video.astype(jnp.float32)
    activated, pullback = jax.vjp(jax.nn.gelu, pre)
    grad_pre = pullback(cotangent.astype(jnp.float32))[0]
    grad_bf = grad_pre.astype(jnp.bfloat16)
    out_grad = kernel_grad(padded_s, grad_bf)
    gain_grad = jnp.sum(grad_pre * video.astype(jnp.float32), axis=(0, 1, 2, 3))
    padded_g = pad_columns(padded_2(grad_bf, (("rows", 2),), 1))
    state_grad = adjoint_conv(padded_g, out_kernel)
    local_adjoint = jnp.einsum(
        "tkp,strcp->skrcp", within, state_grad, precision=lax.Precision.HIGHEST
    )
    leading = jnp.exp(cum[0])[None, None, None, :] * local_adjoint[:, 0]
    piece = lax.all_gather(leading[None].astype(jnp.bfloat16), "tm", axis=0, tiled=True).astype(
        jnp.float32
    )
    count = piece.shape[0]
    upto = running
    index = jnp.arange(count, dtype=jnp.int32)
    reach = upto - group_logs - own_running[None, :]
    weight = jnp.where((index > own)[:, None], jnp.exp(jnp.minimum(reach, 0.0)), 0.0)
    back_in = empty + jnp.einsum("np,nsrcp->srcp", weight, piece, precision=lax.Precision.HIGHEST)
    adjoint = (
        local_adjoint
        + jnp.exp(group_total[None, :] - cum)[None, :, None, None, :] * back_in[:, None]
    )
    previous = jnp.concatenate([carry_in[:, None], states[:, :-1]], axis=1)
    decay_part = jnp.sum(
        adjoint * jnp.exp(log_decay)[None, :, None, None, :] * previous, axis=(0, 2, 3)
    )
    decay_scale = 1.0 / math.sqrt(seqs * rows * cols * lax.axis_size("rows") * lax.axis_size("dp"))
    decay_grad = lax.psum(decay_part, ("rows", "dp")) * decay_scale
    adjoint_bf = adjoint.astype(jnp.bfloat16)
    in_grad = kernel_grad(padded_x, adjoint_bf)
    padded_a = pad_columns(padded_2(adjoint_bf, (("rows", 2),), 1))
    video_grad = (adjoint_conv(padded_a, in_kernel) + skip_gain * grad_pre).astype(jnp.bfloat16)
    in_sum, out_sum, gain_sum = lax.psum((in_grad, out_grad, gain_grad), ("tm", "rows", "dp"))
    weight_scale = 1.0 / math.sqrt(
        seqs
        * frames
        * rows
        * cols
        * lax.axis_size("tm")
        * lax.axis_size("rows")
        * lax.axis_size("dp")
    )
    return (
        activated.astype(jnp.bfloat16),
        video_grad,
        in_sum * weight_scale,
        out_sum * weight_scale,
        gain_sum * weight_scale,
        decay_grad,
    )


def solution(mesh):
    placed = (
        P("dp", "tm", "rows", None, None),
        P("dp", "tm", "rows", None, None),
        P(),
        P(),
        P(),
        P("tm", None),
    )
    return jax.shard_map(
        on_device,
        mesh=mesh,
        in_specs=placed,
        out_specs=(
            P("dp", "tm", "rows", None, None),
            P("dp", "tm", "rows", None, None),
            P(),
            P(),
            P(),
            P("tm", None),
        ),
        check_vma=False,
    )
```

profile of v0, /device:TPU:0, one launch (start us, length us, event | category | flops | bytes accessed | tf_op | source)
XLA Modules:
  0.0 367.8 jit_solution(14901978521855251328)
XLA Ops:
  7.2 1.0 fusion.177
  8.2 5.0 %collective-permute-start = (bf16[1,16,1,32,128]{4,3,2,1,0:T(8,128)(2,1)S(1)}, bf16[1,16,1,32,128]{4,3,2,1,0:T(8,128)(2,1)S(1)}, u32[]{:S(2)}, u32[]{:S(2)}) collective-permute-start(bf16[1,16,1,32,128]{4,3,2,1,0:T(8,128)(2,1)S(1)} %get-tuple-element.71), channel_id=1, source_target_pairs={{0,4},{4,8},{8,12},{1,5},{5,9},{9,13},{2,6},{6,10},{10,14},{3,7},{... | collective-permute-start | bytes 393224 | tf_op jit(solution)/shard_map/ppermute | solution.py:16
  13.2 1.3 collective-permute-start.1
  15.2 4.2 %all-gather = f32[2,1,128]{2,1,0:T(1,128)S(1)} all-gather(f32[1,1,128]{2,1,0:T(1,128)S(1)} %slice_bitcast_fusion.1), channel_id=1, replica_groups=mesh['tm'=2,'rows'=4,'dp'=4] {'tm'}, dimensions={0}, use_global_device_ids=true | all-gather | bytes 1536 | tf_op jit(solution)/shard_map/all_gather | solution.py:87
  20.0 1.6 fusion.25
  25.6 4.5 %copy.169 = f32[16,4,32,128]{2,0,1,3:T(8,128)} copy(f32[16,4,32,128]{3,2,1,0:T(8,128)S(1)} %bitcast.443) | data formatting | bytes 2097152 | tf_op jit(solution)/shard_map/reshape
  30.1 8.3 %fusion.19 = f32[128,4,32,16]{2,3,1,0:T(8,128)} fusion(f32[16,4,32,128]{2,0,1,3:T(8,128)} %copy.169, f32[16,128]{0,1:T(8,128)S(1)} %copy.167, pred[16,16]{0,1:T(8,128)(4,1)S(1)} %iota_compare_fusion.2), kind=kOutput, calls=%fused_computation.74 | convolution fusion | flops 50429952 | bytes 2105600 | tf_op jit(solution)/shard_map/tkp,skrcp->strcp/dot_general | solution.py:84
  38.4 3.7 %copy.171 = f32[128,4,32,16]{0,2,1,3:T(8,128)S(1)} copy(f32[128,4,32,16]{2,3,1,0:T(8,128)} %fusion.19) | data formatting | bytes 2097152 | tf_op jit(solution)/shard_map/tkp,skrcp->strcp/dot_general | solution.py:84
  42.1 4.6 %all_gather.9 = bf16[2,1,4,32,128]{4,3,2,1,0:T(8,128)(2,1)S(1)} all-gather(bf16[1,1,4,32,128]{4,3,2,1,0:T(8,128)(2,1)S(1)} %slice.550), channel_id=1, replica_groups=mesh['tm'=2,'rows'=4,'dp'=4] {'tm'}, dimensions={0}, use_global_device_ids=true | all-gather | bytes 98304 | tf_op jit(solution)/shard_map/all_gather | solution.py:91
  47.0 4.2 %collective-permute-start.2 = (bf16[1,16,1,32,128]{4,3,2,1,0:T(8,128)(2,1)S(1)}, bf16[1,16,1,32,128]{4,3,2,1,0:T(8,128)(2,1)S(1)}, u32[]{:S(2)}, u32[]{:S(2)}) collective-permute-start(bf16[1,16,1,32,128]{4,3,2,1,0:T(8,128)(2,1)S(1)} %get-tuple-element.67), channel_id=1, source_target_pairs={{0,4},{4,8},{8,12},{1,5},{5,9},{9,13},{2,6},{6,10},{10,14},{3,7},{... | collective-permute-start | bytes 393224 | tf_op jit(solution)/shard_map/ppermute | solution.py:16
  51.2 1.5 collective-permute-start.3
  52.7 1.1 slice.347
  53.9 4.2 %collective-permute-done.3 = bf16[1,16,1,32,128]{4,3,2,1,0:T(8,128)(2,1)S(1)} collective-permute-done((bf16[1,16,1,32,128]{4,3,2,1,0:T(8,128)(2,1)S(1)}, bf16[1,16,1,32,128]{4,3,2,1,0:T(8,128)(2,1)S(1)}, u32[]{:S(2)}, u32[]{:S(2)}) %collective-permute-start.3) | collective-permute-done | bytes 131104 | tf_op jit(solution)/shard_map/ppermute | solution.py:18
  62.9 1.8 fusion.6
  64.8 1.0 convolution_bitcast_fusion.4
  65.8 1.0 convolution_bitcast_fusion.1
  66.7 1.0 convolution_bitcast_fusion.7
  67.7 1.0 convolution_bitcast_fusion.5
  68.7 1.0 convolution_bitcast_fusion.3
  69.7 1.0 convolution_bitcast_fusion.2
  70.6 1.0 convolution_bitcast_fusion
  71.6 1.0 convolution_bitcast_fusion.8
  72.5 1.0 convolution_bitcast_fusion.6
  74.2 40.4 %psum.30 = f32[128]{0:T(128)S(1)} all-reduce(f32[128]{0:T(128)S(1)} %get-tuple-element.26), channel_id=1, replica_groups=mesh['tm'=2,'rows'=4,'dp'=4] {'tm','rows','dp'}, use_global_device_ids=true, to_apply=%region_5.6 | all-reduce | flops 128 | bytes 1024 | tf_op jit(solution)/shard_map/psum | solution.py:138
  115.1 2.2 collective-permute-start.4
  117.3 1.5 collective-permute-start.5
  118.8 0.9 maximum_bitcast_fusion.4
  119.7 0.9 maximum_bitcast_fusion.5
  122.4 1.9 collective-permute-done.5
  127.9 1.3 fusion.1
  129.2 5.4 %copy.172 = f32[16,4,32,128]{2,0,1,3:T(8,128)} copy(f32[16,4,32,128]{3,2,1,0:T(8,128)} %bitcast.442) | data formatting | bytes 2097152 | tf_op jit(solution)/shard_map/reshape.7
  134.6 8.1 %fusion.17 = f32[128,4,32,16]{2,3,1,0:T(8,128)} fusion(f32[16,4,32,128]{2,0,1,3:T(8,128)} %copy.172, f32[16,128]{0,1:T(8,128)S(1)} %copy.167, pred[16,16]{0,1:T(8,128)(4,1)S(1)} %iota_compare_fusion.2), kind=kOutput, calls=%fused_computation.72 | convolution fusion | flops 50429952 | bytes 2105600 | tf_op jit(solution)/shard_map/tkp,strcp->skrcp/dot_general | solution.py:111
  142.8 4.5 %copy.173 = f32[128,4,32,16]{0,2,1,3:T(8,128)} copy(f32[128,4,32,16]{2,3,1,0:T(8,128)} %fusion.17) | data formatting | bytes 2097152 | tf_op jit(solution)/shard_map/tkp,strcp->skrcp/dot_general | solution.py:111
  148.2 5.1 %all_gather.11 = bf16[2,1,4,32,128]{4,3,2,1,0:T(8,128)(2,1)S(1)} all-gather(bf16[1,1,4,32,128]{4,3,2,1,0:T(8,128)(2,1)S(1)} %fusion.71), channel_id=1, replica_groups=mesh['tm'=2,'rows'=4,'dp'=4] {'tm'}, dimensions={0}, use_global_device_ids=true | all-gather | bytes 98304 | tf_op jit(solution)/shard_map/all_gather | solution.py:115
  153.3 1.9 fusion.16
  155.9 1.0 convolution_bitcast_fusion.14
  157.6 1.0 convolution_bitcast_fusion.11
  158.6 1.0 convolution_bitcast_fusion.9
  159.5 1.0 convolution_bitcast_fusion.17
  160.5 1.0 convolution_bitcast_fusion.15
  161.6 57.8 %psum.31 = f32[16,128]{0,1:T(8,128)S(1)} all-reduce(f32[16,128]{0,1:T(8,128)S(1)} %copy.212), channel_id=1, replica_groups=mesh['tm'=2,'rows'=4,'dp'=4] {'rows','dp'}, use_global_device_ids=true, to_apply=%region_7.8 | all-reduce | flops 2048 | bytes 16384 | tf_op jit(solution)/shard_map/psum | solution.py:133
  219.4 1.3 collective-permute-start.6
  220.7 1.3 collective-permute-start.7
  225.4 2.2 collective-permute-done.7
  231.8 1.0 add_convert_fusion
  232.8 124.3 %all-reduce.7.cloned.1.call-done = (f32[3,3,128,128]{3,2,1,0:T(8,128)}, f32[3,3,128,128]{3,2,1,0:T(8,128)}) async-done(((f32[3,3,128,128]{3,2,1,0:T(8,128)}, f32[3,3,128,128]{3,2,1,0:T(8,128)}), (f32[3,3,128,128]{3,2,1,0:T(8,128)}, f32[3,3,128,128]{3,2,1,0:T(8,128)})) %all-reduce.7.cloned.1.call-update) | async-done | bytes 1179664 | tf_op jit(solution)/shard_map/psum | solution.py:138
  357.2 1.9 broadcast_multiply_fusion.1
  359.1 1.9 broadcast_multiply_fusion
  (110 shorter events, 26.8 us)
Async XLA Ops:
  7.2 350.0 %all-reduce.7.cloned.1.call-start = ((), (), s32[]{:S(2)}) async-start(), calls=%async_computation | async-start | bytes 2359296 | tf_op jit(solution)/shard_map/psum | solution.py:138
  8.2 11.5 %collective-permute-start = (bf16[1,16,1,32,128]{4,3,2,1,0:T(8,128)(2,1)S(1)}, bf16[1,16,1,32,128]{4,3,2,1,0:T(8,128)(2,1)S(1)}, u32[]{:S(2)}, u32[]{:S(2)}) collective-permute-start(bf16[1,16,1,32,128]{4,3,2,1,0:T(8,128)(2,1)S(1)} %get-tuple-element.71), channel_id=1, source_target_pairs={{0,4},{4,8},{8,12},{1,5},{5,9},{9,13},{2,6},{6,10},{10,14},{3,7},{... | collective-permute-start | bytes 393224 | tf_op jit(solution)/shard_map/ppermute | solution.py:16
  13.2 6.9 %collective-permute-start.1 = (bf16[1,16,1,32,128]{4,3,2,1,0:T(8,128)(2,1)S(1)}, bf16[1,16,1,32,128]{4,3,2,1,0:T(8,128)(2,1)S(1)}, u32[]{:S(2)}, u32[]{:S(2)}) collective-permute-start(bf16[1,16,1,32,128]{4,3,2,1,0:T(8,128)(2,1)S(1)} %get-tuple-element.72), channel_id=1, source_target_pairs={{4,0},{8,4},{12,8},{5,1},{9,5},{13,9},{6,2},{10,6},{14,10},{7,3},{... | collective-permute-start | bytes 393224 | tf_op jit(solution)/shard_map/ppermute | solution.py:18
  21.7 1.0 copy-start.6
  22.3 1.1 copy-start
  23.4 0.8 copy-start.3
  23.4 1.9 copy-start.1
  42.1 10.6 %copy-start.10 = (f32[16,128]{1,0:T(8,128)S(1)}, f32[16,128]{1,0:T(8,128)}, u32[]{:S(2)}) copy-start(f32[16,128]{1,0:T(8,128)} %param.11) | copy-start | bytes 24580
  47.0 6.9 %collective-permute-start.2 = (bf16[1,16,1,32,128]{4,3,2,1,0:T(8,128)(2,1)S(1)}, bf16[1,16,1,32,128]{4,3,2,1,0:T(8,128)(2,1)S(1)}, u32[]{:S(2)}, u32[]{:S(2)}) collective-permute-start(bf16[1,16,1,32,128]{4,3,2,1,0:T(8,128)(2,1)S(1)} %get-tuple-element.67), channel_id=1, source_target_pairs={{0,4},{4,8},{8,12},{1,5},{5,9},{9,13},{2,6},{6,10},{10,14},{3,7},{... | collective-permute-start | bytes 393224 | tf_op jit(solution)/shard_map/ppermute | solution.py:16
  51.2 6.9 %collective-permute-start.3 = (bf16[1,16,1,32,128]{4,3,2,1,0:T(8,128)(2,1)S(1)}, bf16[1,16,1,32,128]{4,3,2,1,0:T(8,128)(2,1)S(1)}, u32[]{:S(2)}, u32[]{:S(2)}) collective-permute-start(bf16[1,16,1,32,128]{4,3,2,1,0:T(8,128)(2,1)S(1)} %get-tuple-element.68), channel_id=1, source_target_pairs={{4,0},{8,4},{12,8},{5,1},{9,5},{13,9},{6,2},{10,6},{14,10},{7,3},{... | collective-permute-start | bytes 393224 | tf_op jit(solution)/shard_map/ppermute | solution.py:18
  58.6 1.0 copy-start.5
  61.9 1.0 copy-start.8
  61.9 1.0 copy-start.11
  115.1 7.3 %collective-permute-start.4 = (bf16[1,16,1,32,128]{4,3,2,1,0:T(8,128)(2,1)}, bf16[1,16,1,32,128]{4,3,2,1,0:T(8,128)(2,1)S(1)}, u32[]{:S(2)}, u32[]{:S(2)}) collective-permute-start(bf16[1,16,1,32,128]{4,3,2,1,0:T(8,128)(2,1)} %get-tuple-element.63), channel_id=1, source_target_pairs={{0,4},{4,8},{8,12},{1,5},{5,9},{9,13},{2,6},{6,10},{10,14},{3,7},{... | collective-permute-start | bytes 393224 | tf_op jit(solution)/shard_map/ppermute | solution.py:16
  117.3 7.1 %collective-permute-start.5 = (bf16[1,16,1,32,128]{4,3,2,1,0:T(8,128)(2,1)}, bf16[1,16,1,32,128]{4,3,2,1,0:T(8,128)(2,1)S(1)}, u32[]{:S(2)}, u32[]{:S(2)}) collective-permute-start(bf16[1,16,1,32,128]{4,3,2,1,0:T(8,128)(2,1)} %get-tuple-element.64), channel_id=1, source_target_pairs={{4,0},{8,4},{12,8},{5,1},{9,5},{13,9},{6,2},{10,6},{14,10},{7,3},{... | collective-permute-start | bytes 393224 | tf_op jit(solution)/shard_map/ppermute | solution.py:18
  147.3 7.9 %copy-start.2 = (bf16[1,16,4,32,128]{4,3,2,1,0:T(8,128)(2,1)S(1)}, bf16[1,16,4,32,128]{4,3,2,1,0:T(8,128)(2,1)}, u32[]{:S(2)}) copy-start(bf16[1,16,4,32,128]{4,3,2,1,0:T(8,128)(2,1)} %copy-done.1) | copy-start | bytes 1572868
  153.3 2.3 copy-start.4
  160.5 61.5 %copy-start.9 = (f32[1,128,128]{2,1,0:T(8,128)S(1)}, f32[1,128,128]{2,1,0:T(8,128)}, u32[]{:S(2)}) copy-start(f32[1,128,128]{2,1,0:T(8,128)} %convolution_bitcast_fusion.14) | copy-start | bytes 196612
  219.4 6.0 %collective-permute-start.6 = (bf16[1,16,1,32,128]{4,3,2,1,0:T(8,128)(2,1)S(1)}, bf16[1,16,1,32,128]{4,3,2,1,0:T(8,128)(2,1)S(1)}, u32[]{:S(2)}, u32[]{:S(2)}) collective-permute-start(bf16[1,16,1,32,128]{4,3,2,1,0:T(8,128)(2,1)S(1)} %get-tuple-element.59), channel_id=1, source_target_pairs={{0,4},{4,8},{8,12},{1,5},{5,9},{9,13},{2,6},{6,10},{10,14},{3,7},{... | collective-permute-start | bytes 393224 | tf_op jit(solution)/shard_map/ppermute | solution.py:16
  220.7 6.9 %collective-permute-start.7 = (bf16[1,16,1,32,128]{4,3,2,1,0:T(8,128)(2,1)S(1)}, bf16[1,16,1,32,128]{4,3,2,1,0:T(8,128)(2,1)S(1)}, u32[]{:S(2)}, u32[]{:S(2)}) collective-permute-start(bf16[1,16,1,32,128]{4,3,2,1,0:T(8,128)(2,1)S(1)} %get-tuple-element.60), channel_id=1, source_target_pairs={{4,0},{8,4},{12,8},{5,1},{9,5},{13,9},{6,2},{10,6},{14,10},{7,3},{... | collective-permute-start | bytes 393224 | tf_op jit(solution)/shard_map/ppermute | solution.py:18
  228.0 1.0 copy-start.7
Sparse Core Ops, SparseCore 0:
  225.5 131.6 all-reduce.6
where the time goes:
time: 369 us; the launch traced here: 368 us
  waiting for transfers between devices  133 us (36%)
  blocking collectives  112 us (30%)
  matrix products  42.6 us (12%)
  local copies, waits for them, and re-layouts  26.5 us (7%)
  other arithmetic  20.8 us (6%)
  starting transfers between devices  18.3 us (5%)
  between operations  14.6 us (4%)
    psum x1, waiting for transfers between devices, on_device(): lax.psum((in_grad, out_grad, gain_grad), ('tm', 'rows', 'dp'))  124 us
    psum x1, blocking collectives, on_device(): decay_grad = lax.psum(decay_part, ('rows', 'dp')) * decay_scale  57.8 us
    psum x1, blocking collectives, on_device(): lax.psum((in_grad, out_grad, gain_grad), ('tm', 'rows', 'dp'))  40.4 us
    dot_general x18, matrix products, kernel_grad(): lax.dot_general(piece, flat_grad, (((0,), (0,)), ((), ())), preferred_ele...  14.9 us
    ppermute x4, starting transfers between devices, padded_2(): lax.ppermute(tail, axis, [(i, (i + 1) % count) for i in range(ends)])  12.7 us
    ppermute x4, waiting for transfers between devices, padded_2(): lax.ppermute(head, axis, [((i + 1) % count, i) for i in range(ends)])  8.64 us
    dot_general x1, matrix products, on_device(): jnp.einsum('tkp,skrcp->strcp', within, drive, precision=lax.Precision.HIG...  8.27 us
    dot_general x1, matrix products, on_device(): jnp.einsum('tkp,strcp->skrcp', within, state_grad, precision=lax.Precisio...  8.14 us
  transfers between devices with their start and end apart: 9, of which 5 were waited for; matrix products, arithmetic and copies ran while one was open for 4% of the time, Pallas kernels for 0%

commit v1 on v0

--- a/solution.py
+++ b/solution.py
@@ -135,7 +135,9 @@
     in_grad = kernel_grad(padded_x, adjoint_bf)
     padded_a = pad_columns(padded_2(adjoint_bf, (("rows", 2),), 1))
     video_grad = (adjoint_conv(padded_a, in_kernel) + skip_gain * grad_pre).astype(jnp.bfloat16)
-    in_sum, out_sum, gain_sum = lax.psum((in_grad, out_grad, gain_grad), ("tm", "rows", "dp"))
+    in_sum, out_sum, gain_sum = lax.psum(
+        lax.psum((in_grad, out_grad, gain_grad), ("rows", "dp")), "tm"
+    )
     weight_scale = 1.0 / math.sqrt(
         seqs
         * frames

time: 369 us -> 337 us (0.913)
  blocking collectives: 112 us -> 76.9 us
    psum x2, blocking collectives: 98.2 us -> 63.3 us  [the longest x1 58.3 us: on_device(): lax.psum((in_grad, out_grad, gain_grad), ('rows', 'dp'))]
    dot_general x18, matrix products: 14.9 us -> 11.1 us  [kernel_grad(): lax.dot_general(piece, flat_grad, (((0,), (0,)), ((), ())), preferred_ele...]
    psum x1 -> x2, waiting for transfers between devices: 124 us -> 125 us  [the longest x1 84.8 us: on_device(): lax.psum((in_grad, out_grad, gain_grad), ('rows', 'dp'))]
  transfers between devices with their start and end apart: 9 -> 10, of which waited for: 5 -> 6; matrix products, arithmetic and copies ran while one was open for 4% -> 5% of each run, Pallas kernels for 0% -> 0%
where the time goes in v1:
time: 337 us; the launch traced here: 336 us
  waiting for transfers between devices  136 us (40%)
  blocking collectives  76.9 us (23%)
  matrix products  42.2 us (13%)
  local copies, waits for them, and re-layouts  27.8 us (8%)
  starting transfers between devices  19.6 us (6%)
  other arithmetic  18.2 us (5%)
  between operations  14.7 us (4%)
    psum x1, waiting for transfers between devices, on_device(): lax.psum((in_grad, out_grad, gain_grad), ('rows', 'dp'))  84.8 us
    psum x1, blocking collectives, on_device(): lax.psum((in_grad, out_grad, gain_grad), ('rows', 'dp'))  58.3 us
    psum x1, waiting for transfers between devices, on_device(): lax.psum(lax.psum((in_grad, out_grad, gain_grad), ('rows', 'dp')), 'tm')  40.2 us
    ppermute x4, starting transfers between devices, padded_2(): lax.ppermute(tail, axis, [(i, (i + 1) % count) for i in range(ends)])  14 us
    dot_general x18, matrix products, kernel_grad(): lax.dot_general(piece, flat_grad, (((0,), (0,)), ((), ())), preferred_ele...  11.1 us
    ppermute x4, waiting for transfers between devices, padded_2(): lax.ppermute(head, axis, [((i + 1) % count, i) for i in range(ends)])  11.1 us
    dot_general x18, matrix products, adjoint_conv(): lax.dot_general(piece, kernel[i, j], (((1,), (1,)), ((), ())), preferred_...  9.56 us
    dot_general x1, matrix products, on_device(): jnp.einsum('tkp,skrcp->strcp', within, drive, precision=lax.Precision.HIG...  8.31 us
  transfers between devices with their start and end apart: 10, of which 6 were waited for; matrix products, arithmetic and copies ran while one was open for 5% of the time, Pallas kernels for 0%

profile of v1, /device:TPU:0, one launch (start us, length us, event | category | flops | bytes accessed | tf_op | source)
XLA Modules:
  0.0 335.6 jit_solution(17731125966195582412)
XLA Ops:
  7.2 1.0 fusion.177
  8.2 5.0 %collective-permute-start = (bf16[1,16,1,32,128]{4,3,2,1,0:T(8,128)(2,1)S(1)}, bf16[1,16,1,32,128]{4,3,2,1,0:T(8,128)(2,1)S(1)}, u32[]{:S(2)}, u32[]{:S(2)}) collective-permute-start(bf16[1,16,1,32,128]{4,3,2,1,0:T(8,128)(2,1)S(1)} %get-tuple-element.75), channel_id=1, source_target_pairs={{0,4},{4,8},{8,12},{1,5},{5,9},{9,13},{2,6},{6,10},{10,14},{3,7},{... | collective-permute-start | bytes 393224 | tf_op jit(solution)/shard_map/ppermute | solution.py:16
  13.2 1.3 collective-permute-start.1
  15.2 4.2 %all-gather = f32[2,1,128]{2,1,0:T(1,128)S(1)} all-gather(f32[1,1,128]{2,1,0:T(1,128)S(1)} %slice_bitcast_fusion.1), channel_id=1, replica_groups=mesh['tm'=2,'rows'=4,'dp'=4] {'tm'}, dimensions={0}, use_global_device_ids=true | all-gather | bytes 1536 | tf_op jit(solution)/shard_map/all_gather | solution.py:87
  20.0 1.6 fusion.25
  25.6 4.5 %copy.169 = f32[16,4,32,128]{2,0,1,3:T(8,128)} copy(f32[16,4,32,128]{3,2,1,0:T(8,128)S(1)} %bitcast.443) | data formatting | bytes 2097152 | tf_op jit(solution)/shard_map/reshape
  30.1 8.3 %fusion.19 = f32[128,4,32,16]{2,3,1,0:T(8,128)} fusion(f32[16,4,32,128]{2,0,1,3:T(8,128)} %copy.169, f32[16,128]{0,1:T(8,128)S(1)} %copy.167, pred[16,16]{0,1:T(8,128)(4,1)S(1)} %iota_compare_fusion.2), kind=kOutput, calls=%fused_computation.74 | convolution fusion | flops 50429952 | bytes 2105600 | tf_op jit(solution)/shard_map/tkp,skrcp->strcp/dot_general | solution.py:84
  38.4 3.7 %copy.171 = f32[128,4,32,16]{0,2,1,3:T(8,128)S(1)} copy(f32[128,4,32,16]{2,3,1,0:T(8,128)} %fusion.19) | data formatting | bytes 2097152 | tf_op jit(solution)/shard_map/tkp,skrcp->strcp/dot_general | solution.py:84
  42.2 4.6 %all_gather.9 = bf16[2,1,4,32,128]{4,3,2,1,0:T(8,128)(2,1)S(1)} all-gather(bf16[1,1,4,32,128]{4,3,2,1,0:T(8,128)(2,1)S(1)} %slice.550), channel_id=1, replica_groups=mesh['tm'=2,'rows'=4,'dp'=4] {'tm'}, dimensions={0}, use_global_device_ids=true | all-gather | bytes 98304 | tf_op jit(solution)/shard_map/all_gather | solution.py:91
  47.0 4.2 %collective-permute-start.2 = (bf16[1,16,1,32,128]{4,3,2,1,0:T(8,128)(2,1)S(1)}, bf16[1,16,1,32,128]{4,3,2,1,0:T(8,128)(2,1)S(1)}, u32[]{:S(2)}, u32[]{:S(2)}) collective-permute-start(bf16[1,16,1,32,128]{4,3,2,1,0:T(8,128)(2,1)S(1)} %get-tuple-element.71), channel_id=1, source_target_pairs={{0,4},{4,8},{8,12},{1,5},{5,9},{9,13},{2,6},{6,10},{10,14},{3,7},{... | collective-permute-start | bytes 393224 | tf_op jit(solution)/shard_map/ppermute | solution.py:16
  51.2 1.5 collective-permute-start.3
  52.7 1.1 slice.347
  53.9 4.2 %collective-permute-done.3 = bf16[1,16,1,32,128]{4,3,2,1,0:T(8,128)(2,1)S(1)} collective-permute-done((bf16[1,16,1,32,128]{4,3,2,1,0:T(8,128)(2,1)S(1)}, bf16[1,16,1,32,128]{4,3,2,1,0:T(8,128)(2,1)S(1)}, u32[]{:S(2)}, u32[]{:S(2)}) %collective-permute-start.3) | collective-permute-done | bytes 131104 | tf_op jit(solution)/shard_map/ppermute | solution.py:18
  63.0 1.8 fusion.6
  68.0 3.5 %collective-permute-start.4 = (bf16[1,16,1,32,128]{4,3,2,1,0:T(8,128)(2,1)S(1)}, bf16[1,16,1,32,128]{4,3,2,1,0:T(8,128)(2,1)S(1)}, u32[]{:S(2)}, u32[]{:S(2)}) collective-permute-start(bf16[1,16,1,32,128]{4,3,2,1,0:T(8,128)(2,1)S(1)} %get-tuple-element.67), channel_id=1, source_target_pairs={{0,4},{4,8},{8,12},{1,5},{5,9},{9,13},{2,6},{6,10},{10,14},{3,7},{... | collective-permute-start | bytes 393224 | tf_op jit(solution)/shard_map/ppermute | solution.py:16
  71.5 1.5 collective-permute-start.5
  74.0 4.4 %collective-permute-done.5 = bf16[1,16,1,32,128]{4,3,2,1,0:T(8,128)(2,1)S(1)} collective-permute-done((bf16[1,16,1,32,128]{4,3,2,1,0:T(8,128)(2,1)S(1)}, bf16[1,16,1,32,128]{4,3,2,1,0:T(8,128)(2,1)S(1)}, u32[]{:S(2)}, u32[]{:S(2)}) %collective-permute-start.5) | collective-permute-done | bytes 131104 | tf_op jit(solution)/shard_map/ppermute | solution.py:18
  82.0 1.3 fusion.1
  83.3 5.4 %copy.172 = f32[16,4,32,128]{2,0,1,3:T(8,128)} copy(f32[16,4,32,128]{3,2,1,0:T(8,128)} %bitcast.442) | data formatting | bytes 2097152 | tf_op jit(solution)/shard_map/reshape.7
  88.7 8.2 %fusion.17 = f32[128,4,32,16]{2,3,1,0:T(8,128)} fusion(f32[16,4,32,128]{2,0,1,3:T(8,128)} %copy.172, f32[16,128]{0,1:T(8,128)S(1)} %copy.167, pred[16,16]{0,1:T(8,128)(4,1)S(1)} %iota_compare_fusion.2), kind=kOutput, calls=%fused_computation.72 | convolution fusion | flops 50429952 | bytes 2105600 | tf_op jit(solution)/shard_map/tkp,strcp->skrcp/dot_general | solution.py:111
  96.9 4.5 %copy.173 = f32[128,4,32,16]{0,2,1,3:T(8,128)} copy(f32[128,4,32,16]{2,3,1,0:T(8,128)} %fusion.17) | data formatting | bytes 2097152 | tf_op jit(solution)/shard_map/tkp,strcp->skrcp/dot_general | solution.py:111
  101.4 0.9 fusion.71
  102.3 4.8 %all_gather.11 = bf16[2,1,4,32,128]{4,3,2,1,0:T(8,128)(2,1)S(1)} all-gather(bf16[1,1,4,32,128]{4,3,2,1,0:T(8,128)(2,1)S(1)} %fusion.71), channel_id=1, replica_groups=mesh['tm'=2,'rows'=4,'dp'=4] {'tm'}, dimensions={0}, use_global_device_ids=true | all-gather | bytes 98304 | tf_op jit(solution)/shard_map/all_gather | solution.py:115
  107.2 1.9 fusion.16
  109.0 1.0 convolution_bitcast_fusion.10
  110.0 1.0 convolution_bitcast_fusion.16
  111.0 1.0 convolution_bitcast_fusion.14
  111.9 1.0 convolution_bitcast_fusion.13
  113.2 1.0 convolution_bitcast_fusion.11
  114.2 1.0 convolution_bitcast_fusion.9
  115.2 1.0 convolution_bitcast_fusion.17
  116.2 1.0 convolution_bitcast_fusion.15
  117.2 58.3 %all-reduce.4 = (f32[128]{0:T(128)S(1)}, f32[16,128]{0,1:T(8,128)S(1)}) all-reduce(f32[128]{0:T(128)S(1)} %get-tuple-element.30, f32[16,128]{0,1:T(8,128)S(1)} %copy.212), channel_id=1, replica_groups=mesh['tm'=2,'rows'=4,'dp'=4] {'rows','dp'}, use_global_device_ids=true, to_apply=%region_7.8 | all-reduce | flops 2176 | bytes 17408 | tf_op jit(solution)/shard_map/psum | solution.py:139
  175.6 4.9 %psum.54 = f32[128]{0:T(128)S(1)} all-reduce(f32[128]{0:T(128)S(1)} %get-tuple-element.24), channel_id=1, replica_groups=mesh['tm'=2,'rows'=4,'dp'=4] {'tm'}, use_global_device_ids=true, to_apply=%region_8.9 | all-reduce | flops 128 | bytes 1024 | tf_op jit(solution)/shard_map/psum | solution.py:138
  181.2 1.3 collective-permute-start.6
  182.5 1.3 collective-permute-start.7
  183.8 0.9 maximum_bitcast_fusion.2
  184.7 0.9 maximum_bitcast_fusion
  187.1 2.2 collective-permute-done.7
  190.5 1.4 fusion.170
  192.9 1.3 fusion.94
  194.5 1.3 convolution_add_fusion.3
  195.8 84.8 %all-reduce.10.cloned.1.call-done = (f32[3,3,128,128]{3,2,1,0:T(8,128)}, f32[3,3,128,128]{3,2,1,0:T(8,128)}) async-done(((f32[3,3,128,128]{3,2,1,0:T(8,128)}, f32[3,3,128,128]{3,2,1,0:T(8,128)}), (f32[3,3,128,128]{3,2,1,0:T(8,128)}, f32[3,3,128,128]{3,2,1,0:T(8,128)})) %all-reduce.10.cloned.1.call-update) | async-done | bytes 1179664 | tf_op jit(solution)/shard_map/psum | solution.py:139
  280.6 1.5 convolution_add_fusion.2
  283.6 1.0 add_convert_fusion
  284.7 40.2 %all-reduce.12.cloned.1.call-done = (f32[3,3,128,128]{3,2,1,0:T(8,128)}, f32[3,3,128,128]{3,2,1,0:T(8,128)}) async-done(((f32[3,3,128,128]{3,2,1,0:T(8,128)}, f32[3,3,128,128]{3,2,1,0:T(8,128)}), (f32[3,3,128,128]{3,2,1,0:T(8,128)}, f32[3,3,128,128]{3,2,1,0:T(8,128)})) %all-reduce.12.cloned.1.call-update) | async-done | bytes 1179664 | tf_op jit(solution)/shard_map/psum | solution.py:138
  324.9 1.9 broadcast_multiply_fusion.1
  326.8 1.9 broadcast_multiply_fusion
  (123 shorter events, 24.5 us)
Async XLA Ops:
  7.2 273.4 %all-reduce.10.cloned.1.call-start = ((), (), s32[]{:S(2)}) async-start(), calls=%async_computation | async-start | bytes 2359296 | tf_op jit(solution)/shard_map/psum | solution.py:139
  8.2 11.5 %collective-permute-start = (bf16[1,16,1,32,128]{4,3,2,1,0:T(8,128)(2,1)S(1)}, bf16[1,16,1,32,128]{4,3,2,1,0:T(8,128)(2,1)S(1)}, u32[]{:S(2)}, u32[]{:S(2)}) collective-permute-start(bf16[1,16,1,32,128]{4,3,2,1,0:T(8,128)(2,1)S(1)} %get-tuple-element.75), channel_id=1, source_target_pairs={{0,4},{4,8},{8,12},{1,5},{5,9},{9,13},{2,6},{6,10},{10,14},{3,7},{... | collective-permute-start | bytes 393224 | tf_op jit(solution)/shard_map/ppermute | solution.py:16
  13.2 6.9 %collective-permute-start.1 = (bf16[1,16,1,32,128]{4,3,2,1,0:T(8,128)(2,1)S(1)}, bf16[1,16,1,32,128]{4,3,2,1,0:T(8,128)(2,1)S(1)}, u32[]{:S(2)}, u32[]{:S(2)}) collective-permute-start(bf16[1,16,1,32,128]{4,3,2,1,0:T(8,128)(2,1)S(1)} %get-tuple-element.76), channel_id=1, source_target_pairs={{4,0},{8,4},{12,8},{5,1},{9,5},{13,9},{6,2},{10,6},{14,10},{7,3},{... | collective-permute-start | bytes 393224 | tf_op jit(solution)/shard_map/ppermute | solution.py:18
  21.7 1.0 copy-start.9
  22.3 1.1 copy-start
  23.4 0.8 copy-start.4
  23.4 1.9 copy-start.2
  42.1 10.6 %copy-start.15 = (f32[16,128]{1,0:T(8,128)S(1)}, f32[16,128]{1,0:T(8,128)}, u32[]{:S(2)}) copy-start(f32[16,128]{1,0:T(8,128)} %param.11) | copy-start | bytes 24580
  47.0 6.9 %collective-permute-start.2 = (bf16[1,16,1,32,128]{4,3,2,1,0:T(8,128)(2,1)S(1)}, bf16[1,16,1,32,128]{4,3,2,1,0:T(8,128)(2,1)S(1)}, u32[]{:S(2)}, u32[]{:S(2)}) collective-permute-start(bf16[1,16,1,32,128]{4,3,2,1,0:T(8,128)(2,1)S(1)} %get-tuple-element.71), channel_id=1, source_target_pairs={{0,4},{4,8},{8,12},{1,5},{5,9},{9,13},{2,6},{6,10},{10,14},{3,7},{... | collective-permute-start | bytes 393224 | tf_op jit(solution)/shard_map/ppermute | solution.py:16
  51.2 6.9 %collective-permute-start.3 = (bf16[1,16,1,32,128]{4,3,2,1,0:T(8,128)(2,1)S(1)}, bf16[1,16,1,32,128]{4,3,2,1,0:T(8,128)(2,1)S(1)}, u32[]{:S(2)}, u32[]{:S(2)}) collective-permute-start(bf16[1,16,1,32,128]{4,3,2,1,0:T(8,128)(2,1)S(1)} %get-tuple-element.72), channel_id=1, source_target_pairs={{4,0},{8,4},{12,8},{5,1},{9,5},{13,9},{6,2},{10,6},{14,10},{7,3},{... | collective-permute-start | bytes 393224 | tf_op jit(solution)/shard_map/ppermute | solution.py:18
  58.6 1.0 copy-start.8
  61.9 1.0 copy-start.12
  62.0 1.0 copy-start.16
  68.0 6.0 %collective-permute-start.4 = (bf16[1,16,1,32,128]{4,3,2,1,0:T(8,128)(2,1)S(1)}, bf16[1,16,1,32,128]{4,3,2,1,0:T(8,128)(2,1)S(1)}, u32[]{:S(2)}, u32[]{:S(2)}) collective-permute-start(bf16[1,16,1,32,128]{4,3,2,1,0:T(8,128)(2,1)S(1)} %get-tuple-element.67), channel_id=1, source_target_pairs={{0,4},{4,8},{8,12},{1,5},{5,9},{9,13},{2,6},{6,10},{10,14},{3,7},{... | collective-permute-start | bytes 393224 | tf_op jit(solution)/shard_map/ppermute | solution.py:16
  71.5 6.9 %collective-permute-start.5 = (bf16[1,16,1,32,128]{4,3,2,1,0:T(8,128)(2,1)S(1)}, bf16[1,16,1,32,128]{4,3,2,1,0:T(8,128)(2,1)S(1)}, u32[]{:S(2)}, u32[]{:S(2)}) collective-permute-start(bf16[1,16,1,32,128]{4,3,2,1,0:T(8,128)(2,1)S(1)} %get-tuple-element.68), channel_id=1, source_target_pairs={{4,0},{8,4},{12,8},{5,1},{9,5},{13,9},{6,2},{10,6},{14,10},{7,3},{... | collective-permute-start | bytes 393224 | tf_op jit(solution)/shard_map/ppermute | solution.py:18
  101.4 7.6 %copy-start.3 = (bf16[1,16,4,32,128]{4,3,2,1,0:T(8,128)(2,1)S(1)}, bf16[1,16,4,32,128]{4,3,2,1,0:T(8,128)(2,1)}, u32[]{:S(2)}) copy-start(bf16[1,16,4,32,128]{4,3,2,1,0:T(8,128)(2,1)} %copy-done.2) | copy-start | bytes 1572868
  107.1 2.9 copy-start.5
  116.1 67.6 %copy-start.13 = (f32[1,128,128]{2,1,0:T(8,128)S(1)}, f32[1,128,128]{2,1,0:T(8,128)}, u32[]{:S(2)}) copy-start(f32[1,128,128]{2,1,0:T(8,128)} %convolution_bitcast_fusion.13) | copy-start | bytes 196612
  116.2 67.6 %copy-start.14 = (f32[1,128,128]{2,1,0:T(8,128)S(1)}, f32[1,128,128]{2,1,0:T(8,128)}, u32[]{:S(2)}) copy-start(f32[1,128,128]{2,1,0:T(8,128)} %convolution_bitcast_fusion.14) | copy-start | bytes 196612
  181.2 5.9 %collective-permute-start.6 = (bf16[1,16,1,32,128]{4,3,2,1,0:T(8,128)(2,1)S(1)}, bf16[1,16,1,32,128]{4,3,2,1,0:T(8,128)(2,1)S(1)}, u32[]{:S(2)}, u32[]{:S(2)}) collective-permute-start(bf16[1,16,1,32,128]{4,3,2,1,0:T(8,128)(2,1)S(1)} %get-tuple-element.63), channel_id=1, source_target_pairs={{0,4},{4,8},{8,12},{1,5},{5,9},{9,13},{2,6},{6,10},{10,14},{3,7},{... | collective-permute-start | bytes 393224 | tf_op jit(solution)/shard_map/ppermute | solution.py:16
  182.5 6.9 %collective-permute-start.7 = (bf16[1,16,1,32,128]{4,3,2,1,0:T(8,128)(2,1)S(1)}, bf16[1,16,1,32,128]{4,3,2,1,0:T(8,128)(2,1)S(1)}, u32[]{:S(2)}, u32[]{:S(2)}) collective-permute-start(bf16[1,16,1,32,128]{4,3,2,1,0:T(8,128)(2,1)S(1)} %get-tuple-element.64), channel_id=1, source_target_pairs={{4,0},{8,4},{12,8},{5,1},{9,5},{13,9},{6,2},{10,6},{14,10},{7,3},{... | collective-permute-start | bytes 393224 | tf_op jit(solution)/shard_map/ppermute | solution.py:18
  186.5 138.4 %all-reduce.12.cloned.1.call-start = ((), (), s32[]{:S(2)}) async-start(), calls=%async_computation.1 | async-start | bytes 2359296 | tf_op jit(solution)/shard_map/psum | solution.py:138
  189.3 0.6 copy-start.10
  190.5 1.7 copy-start.11
  194.5 86.1 %copy-start.7 = (bf16[1,16,4,32,128]{4,3,2,1,0:T(8,128)(2,1)S(1)}, bf16[1,16,4,32,128]{4,3,2,1,0:T(8,128)(2,1)}, u32[]{:S(2)}) copy-start(bf16[1,16,4,32,128]{4,3,2,1,0:T(8,128)(2,1)} %get-tuple-element.38) | copy-start | bytes 1572868
  195.8 86.3 %copy-start.6 = (bf16[1,16,4,32,128]{4,3,2,1,0:T(8,128)(2,1)S(1)}, bf16[1,16,4,32,128]{4,3,2,1,0:T(8,128)(2,1)}, u32[]{:S(2)}) copy-start(bf16[1,16,4,32,128]{4,3,2,1,0:T(8,128)(2,1)} %get-tuple-element.37) | copy-start | bytes 1572868
  282.1 1.2 copy-start.1
Sparse Core Ops, SparseCore 0:
  186.7 93.8 all-reduce.9
  282.9 41.9 all-reduce.11
